TPU v7x, 32 devices: a whole 2x2x4 slice. The times are simulated.
32 devices in a mesh: dp: 2 (over core), ctx: 4 (over z), tensor: 4 (over y, x).
Axes of the slice: x: 2, y: 2, z: 4, core: 2. Of those that a mesh axis runs over, the one named last changes fastest.
Arguments:
- tokens: bfloat16 [4096, 2048], P(('dp', 'ctx')), may hold values from -6 to 6
- lengths: int32 [2, 13], P('dp'), may hold values from 1 to 819, 2048 in all within a row
- parents: int32 [2, 13], P('dp'), may hold values from 0 to 4, as said below
- w_query: bfloat16 [2048, 2048], P(('dp', 'ctx'), 'tensor'), may hold values from -0.125 to 0.125
- w_key: bfloat16 [2048, 1024], P(('dp', 'ctx'), 'tensor'), may hold values from -0.125 to 0.125
- w_value: bfloat16 [2048, 1024], P(('dp', 'ctx'), 'tensor'), may hold values from -0.125 to 0.125
- w_out: bfloat16 [2048, 2048], P('tensor', ('dp', 'ctx')), may hold values from -1.5 to 1.5
- w_gate: bfloat16 [2048, 6144], P(('dp', 'ctx'), 'tensor'), may hold values from -0.125 to 0.125
- w_up: bfloat16 [2048, 6144], P(('dp', 'ctx'), 'tensor'), may hold values from -0.125 to 0.125
- w_down: bfloat16 [6144, 2048], P('tensor', ('dp', 'ctx')), may hold values from -0.078125 to 0.078125
- gain_attn: bfloat16 [2048], P(('dp', 'ctx')), may hold values from 0.099609375 to 1.8984375
- gain_mlp: bfloat16 [2048], P(('dp', 'ctx')), may hold values from 0.099609375 to 1.8984375
- gain_query: bfloat16 [128], P(('dp', 'ctx')), may hold values from 0.099609375 to 1.8984375
- gain_key: bfloat16 [128], P(('dp', 'ctx')), may hold values from 0.099609375 to 1.8984375
- cotangent: bfloat16 [4096, 2048], P(('dp', 'ctx')), may hold values from -6 to 6
Outputs:
- result: bfloat16 [4096, 2048], P(('dp', 'ctx'))
- grad_tokens: float32 [4096, 2048], P(('dp', 'ctx'))
- grad_query: float32 [2048, 2048], P(('dp', 'ctx'), 'tensor')
- grad_key: float32 [2048, 1024], P(('dp', 'ctx'), 'tensor')
- grad_value: float32 [2048, 1024], P(('dp', 'ctx'), 'tensor')
- grad_out: float32 [2048, 2048], P('tensor', ('dp', 'ctx'))
- grad_gate: float32 [2048, 6144], P(('dp', 'ctx'), 'tensor')
- grad_up: float32 [2048, 6144], P(('dp', 'ctx'), 'tensor')
- grad_down: float32 [6144, 2048], P('tensor', ('dp', 'ctx'))
- grad_gain_attn: float32 [2048], P(('dp', 'ctx'))
- grad_gain_mlp: float32 [2048], P(('dp', 'ctx'))
- grad_gain_query: float32 [128], P(('dp', 'ctx'))
- grad_gain_key: float32 [128], P(('dp', 'ctx'))
Inputs may be any that keep to these rules, and one draw needn't show every extreme that they name: lengths[t, s] counts the tokens of segment s of tree t; the segments lie in order and each tree's lengths sum to 2048. parents[t, s] is the segment from which segment s of tree t hangs; segments 0 to 4 name 0 (segment 0 is the root), segments 5 to 12 name one of 1 to 4.
All inputs are finite; a program needn't handle non-finite values.
Results may differ from a plain program's by a relative error of at most 0.02.
Values may be sent and summed in bfloat16 or wider, within the bound.
No kernel may reach another device: no remote copies, remote signals or barrier semaphores. Data moves between devices by JAX's collectives and lax.ppermute only.
A program may use at most 192 MiB of HBM per device.

v0:
```python
import math
import jax
import jax.numpy as jnp
from jax import lax
from jax.sharding import PartitionSpec as P

HEAD_DIM = 128
EPS = 1e-06
THETA = 1000000.0
PRECISE = lax.Precision.HIGHEST
BF = jnp.bfloat16
F32 = jnp.float32
ROWS = ("dp", "ctx")


def row_scales(values):
    return lax.rsqrt(jnp.mean(values * values, axis=-1, keepdims=True) + EPS)


def norm_back(grad_in, values, gain_vec, scales):
    upstream = grad_in * gain_vec
    inner_mean = jnp.mean(upstream * values, axis=-1, keepdims=True)
    return (
        scales * upstream - values * scales * scales * scales * inner_mean,
        grad_in * values * scales,
    )


def rotate_pairs(values, cosine, sine_vals):
    half_dim = values.shape[-1] // 2
    first_half = values[..., :half_dim]
    second_half = values[..., half_dim:]
    return jnp.concatenate(
        [
            first_half * cosine - second_half * sine_vals,
            second_half * cosine + first_half * sine_vals,
        ],
        axis=-1,
    )


def rotate_back(values, cosine, sine_vals):
    return rotate_pairs(values, cosine, -sine_vals)


def dot(left, right):
    return jnp.dot(left, right, preferred_element_type=F32)


def inner_rows(left, right):
    return lax.dot_general(left, right, (((0,), (0,)), ((), ())), preferred_element_type=F32)


def outer_cols(left, right):
    return lax.dot_general(left, right, (((1,), (1,)), ((), ())), preferred_element_type=F32)


def swap(values, axis, mask):
    size = lax.axis_size(axis)
    return lax.ppermute(values, axis, [(a, a ^ mask) for a in range(size)])


def scatter_sum(partial):
    size = lax.axis_size("tensor")
    chunk = partial.shape[0] // size
    low = partial.astype(BF)
    total = partial[:chunk]
    for mask in range(1, size):
        total = total + swap(low[mask * chunk : (mask + 1) * chunk], "tensor", mask).astype(F32)
    return total


def gather_rows(own):
    size = lax.axis_size("tensor")
    return [own] + [swap(own, "tensor", mask) for mask in range(1, size)]


def xor_order(values):
    size = lax.axis_size("tensor")
    me = lax.axis_index("tensor")
    chunk = values.shape[0] // size
    return jnp.concatenate(
        [
            lax.dynamic_slice_in_dim(values, (me ^ mask) * chunk, chunk, axis=0)
            for mask in range(size)
        ],
        axis=0,
    )


def grad_scatter(left, right):
    half = left.shape[1] // 2
    me = lax.axis_index("dp")
    theirs = lax.dynamic_slice_in_dim(left, (1 - me) * half, half, axis=1)
    mine = lax.dynamic_slice_in_dim(left, me * half, half, axis=1)
    sent = swap(inner_rows(theirs, right).astype(BF), "dp", 1)
    both = (inner_rows(mine, right) + sent.astype(F32)).astype(BF)
    return lax.psum_scatter(both, "ctx", scatter_dimension=0, tiled=True)


def tree_layout(lengths, parents, tree_total):
    seg_count = lengths.shape[0]
    index = jnp.arange(seg_count, dtype=jnp.int32)
    direct = ((parents[:, None] == index[None, :]) & (parents[:, None] != index[:, None])).astype(
        F32
    )
    reach = direct
    for closure_step in range(4):
        reach = jnp.minimum(reach + jnp.dot(reach, reach, precision=PRECISE), 1.0)
    ends = jnp.cumsum(lengths, dtype=jnp.int32)
    starts = ends - lengths
    offset = jnp.dot(reach, lengths.astype(F32), precision=PRECISE)
    return (starts, reach, offset)


def segment_onehot(places, starts):
    index = jnp.arange(starts.shape[0], dtype=jnp.int32)
    member = (starts[None, :] <= places[:, None]).astype(jnp.int32)
    segment_ids = jnp.sum(member, axis=1, dtype=jnp.int32) - 1
    return (segment_ids, (segment_ids[:, None] == index[None, :]).astype(F32))


def on_device(
    tokens,
    lengths,
    parents,
    w_query,
    w_key,
    w_value,
    w_out,
    w_gate,
    w_up,
    w_down,
    gain_attn,
    gain_mlp,
    gain_query,
    gain_key,
    cotangent,
):
    row_count, width = tokens.shape
    ctx_size = lax.axis_size("ctx")
    split = lax.axis_size("tensor")
    me_t = lax.axis_index("tensor")
    chunk = row_count // split
    tree_total = row_count * ctx_size
    q_cols, k_cols = (w_query.shape[1], w_key.shape[1])
    w_qkv = lax.all_gather(
        jnp.concatenate([w_query, w_key, w_value], axis=1), ROWS, axis=0, tiled=True
    )
    wo_t = lax.all_gather(w_out.T, ROWS, axis=0, tiled=True)
    wg_full = lax.all_gather(w_gate, ROWS, axis=0, tiled=True)
    wu_full = lax.all_gather(w_up, ROWS, axis=0, tiled=True)
    wd_t = lax.all_gather(w_down.T, ROWS, axis=0, tiled=True)
    gain_sizes = (gain_attn.shape[0], gain_mlp.shape[0], gain_query.shape[0], gain_key.shape[0])
    gains = lax.all_gather(
        jnp.concatenate([gain_attn, gain_mlp, gain_query, gain_key])[None], ROWS, axis=0, tiled=True
    ).astype(F32)
    gain_parts, place = ([], 0)
    for size in gain_sizes:
        gain_parts.append(gains[:, place : place + size].reshape(-1))
        place += size
    gain_one, gain_two, gain_q, gain_k = gain_parts
    local = jnp.arange(row_count, dtype=jnp.int32)
    natural = (local // chunk ^ me_t) * chunk + local % chunk
    place_here = lax.axis_index("ctx") * row_count + natural
    place_all = (
        jnp.arange(ctx_size, dtype=jnp.int32)[:, None] * row_count + natural[None, :]
    ).reshape(-1)
    starts, reach, offset = tree_layout(lengths[0], parents[0], tree_total)
    segment_here, onehot_here = segment_onehot(place_here, starts)
    segment_all, onehot_all = segment_onehot(place_all, starts)
    position = place_here.astype(F32) + jnp.dot(
        onehot_here, offset - starts.astype(F32), precision=PRECISE
    )
    ancestor = (
        jnp.dot(jnp.dot(onehot_here, reach, precision=PRECISE), onehot_all.T, precision=PRECISE)
        > 0.5
    )
    allowed = (segment_here[:, None] == segment_all[None, :]) & (
        place_all[None, :] <= place_here[:, None]
    ) | ancestor
    half_dim = HEAD_DIM // 2
    frequency = jnp.exp(jnp.arange(half_dim, dtype=F32) * (-2.0 * math.log(THETA) / HEAD_DIM))
    angles = position[:, None] * frequency[None, :]
    cosine = jnp.cos(angles)[:, None, :]
    sine_vals = jnp.sin(angles)[:, None, :]
    score_scale = 1.0 / math.sqrt(HEAD_DIM)
    x_low = xor_order(tokens)
    g_low = xor_order(cotangent)
    inputs = x_low.astype(F32)
    scale_one = row_scales(inputs)
    normed_attn = (inputs * scale_one * gain_one).astype(BF)
    qkv = dot(normed_attn, w_qkv)
    heads_here = q_cols // HEAD_DIM
    kv_here = k_cols // HEAD_DIM
    group_size = heads_here // kv_here
    q_heads = qkv[:, :q_cols].reshape(row_count, heads_here, HEAD_DIM)
    k_heads = qkv[:, q_cols : q_cols + k_cols].reshape(row_count, kv_here, HEAD_DIM)
    v_bf = qkv[:, q_cols + k_cols :].astype(BF)
    q_scales, k_scales = (row_scales(q_heads), row_scales(k_heads))
    q_bf = rotate_pairs(q_heads * q_scales * gain_q, cosine, sine_vals).astype(BF)
    k_bf = rotate_pairs(k_heads * k_scales * gain_k, cosine, sine_vals).astype(BF)
    kv_all = lax.all_gather(
        jnp.concatenate([k_bf.reshape(row_count, k_cols), v_bf], axis=1), "ctx", axis=0, tiled=True
    )
    k_all = kv_all[:, :k_cols].reshape(tree_total, kv_here, HEAD_DIM)
    v_all = kv_all[:, k_cols:].reshape(tree_total, kv_here, HEAD_DIM)
    q_grouped = q_bf.reshape(row_count, kv_here, group_size, HEAD_DIM)
    scores = (
        jnp.einsum("tkgd,skd->kgts", q_grouped, k_all, preferred_element_type=F32) * score_scale
    )
    scores = jnp.where(allowed[None, None], scores, -1e30)
    row_max = jnp.max(scores, axis=-1, keepdims=True)
    weights = jnp.exp(scores - row_max)
    prob_all = weights / jnp.sum(weights, axis=-1, keepdims=True)
    prob_bf = prob_all.astype(BF)
    mixture = jnp.einsum("kgts,skd->tkgd", prob_bf, v_all, preferred_element_type=F32)
    mixture_bf = mixture.reshape(row_count, heads_here * HEAD_DIM).astype(BF)
    own_inputs = inputs[:chunk]
    hidden = own_inputs + scatter_sum(outer_cols(mixture_bf, wo_t))
    scale_two = row_scales(hidden)
    normed_own = (hidden * scale_two * gain_two).astype(BF)
    normed_mlp = jnp.concatenate(gather_rows(normed_own), axis=0)
    gate_pre = dot(normed_mlp, wg_full)
    up_pre = dot(normed_mlp, wu_full)
    gate_sig = jax.nn.sigmoid(gate_pre)
    gate_act = gate_pre * gate_sig
    inner_bf = (gate_act * up_pre).astype(BF)
    grad_down_t = grad_scatter(g_low, inner_bf)
    grad_inner = dot(g_low, wd_t)
    grad_gate_pre = (grad_inner * up_pre * gate_sig * (1.0 + gate_pre * (1.0 - gate_sig))).astype(
        BF
    )
    grad_up_pre = (grad_inner * gate_act).astype(BF)
    grad_normed_mlp = scatter_sum(
        outer_cols(grad_gate_pre, wg_full) + outer_cols(grad_up_pre, wu_full)
    )
    grad_gate = grad_scatter(normed_mlp, grad_gate_pre)
    grad_up = grad_scatter(normed_mlp, grad_up_pre)
    own_cotangent = g_low[:chunk].astype(F32)
    grad_hidden_norm, gain_two_terms = norm_back(grad_normed_mlp, hidden, gain_two, scale_two)
    gain_two_part = jnp.sum(gain_two_terms, axis=0)
    grad_hidden = own_cotangent + grad_hidden_norm
    grad_attn_bf = jnp.concatenate(gather_rows(grad_hidden.astype(BF)), axis=0)
    result_own = (hidden + scatter_sum(outer_cols(inner_bf, wd_t))).astype(BF)
    result = xor_order(jnp.concatenate(gather_rows(result_own), axis=0))
    grad_out_t = grad_scatter(grad_attn_bf, mixture_bf)
    grad_mixture = (
        dot(grad_attn_bf, wo_t).astype(BF).reshape(row_count, kv_here, group_size, HEAD_DIM)
    )
    grad_probs = jnp.einsum("tkgd,skd->kgts", grad_mixture, v_all, preferred_element_type=F32)
    grad_v_all = jnp.einsum("kgts,tkgd->skd", prob_bf, grad_mixture, preferred_element_type=F32)
    row_total = jnp.sum(prob_all * grad_probs, axis=-1, keepdims=True)
    grad_scores = (prob_all * (grad_probs - row_total)).astype(BF)
    grad_q = (
        jnp.einsum("kgts,skd->tkgd", grad_scores, k_all, preferred_element_type=F32) * score_scale
    )
    grad_k_all = (
        jnp.einsum("kgts,tkgd->skd", grad_scores, q_grouped, preferred_element_type=F32)
        * score_scale
    )
    grad_kv = lax.psum_scatter(
        jnp.concatenate(
            [grad_k_all.reshape(tree_total, k_cols), grad_v_all.reshape(tree_total, k_cols)], axis=1
        ).astype(BF),
        "ctx",
        scatter_dimension=0,
        tiled=True,
    )
    grad_q = grad_q.reshape(row_count, heads_here, HEAD_DIM)
    grad_k = grad_kv[:, :k_cols].reshape(row_count, kv_here, HEAD_DIM).astype(F32)
    grad_v_bf = grad_kv[:, k_cols:]
    grad_q_heads, q_gain_terms = norm_back(
        rotate_back(grad_q, cosine, sine_vals), q_heads, gain_q, q_scales
    )
    grad_k_heads, k_gain_terms = norm_back(
        rotate_back(grad_k, cosine, sine_vals), k_heads, gain_k, k_scales
    )
    grad_qkv_raw = jnp.concatenate(
        [
            grad_q_heads.reshape(row_count, q_cols).astype(BF),
            grad_k_heads.reshape(row_count, k_cols).astype(BF),
            grad_v_bf,
        ],
        axis=1,
    )
    grad_qkv = grad_scatter(normed_attn, grad_qkv_raw)
    partial_back = outer_cols(grad_qkv_raw, w_qkv)
    gain_one_part = jnp.sum(partial_back * inputs * scale_one, axis=0)
    grad_normed_attn = scatter_sum(partial_back)
    grad_input_norm, unused_terms = norm_back(
        grad_normed_attn, own_inputs, gain_one, scale_one[:chunk]
    )
    grad_own = lax.optimization_barrier((grad_hidden + grad_input_norm).astype(BF))
    grad_tokens = xor_order(jnp.concatenate(gather_rows(grad_own), axis=0)).astype(F32)
    block = lax.axis_index("dp") * ctx_size + lax.axis_index("ctx")
    summed = lax.psum(
        jnp.concatenate(
            [
                gain_one_part,
                gain_two_part,
                jnp.sum(q_gain_terms, axis=(0, 1)),
                jnp.sum(k_gain_terms, axis=(0, 1)),
            ]
        ),
        ("dp", "ctx", "tensor"),
    )
    gain_grads, place = ([], 0)
    for size, part in zip(gain_sizes, gain_parts):
        gain_grads.append(lax.dynamic_slice_in_dim(summed, place + block * size, size))
        place += part.shape[0]
    return (
        result,
        grad_tokens,
        grad_qkv[:, :q_cols].astype(F32),
        grad_qkv[:, q_cols : q_cols + k_cols].astype(F32),
        grad_qkv[:, q_cols + k_cols :].astype(F32),
        grad_out_t.T.astype(F32),
        grad_gate.astype(F32),
        grad_up.astype(F32),
        grad_down_t.T.astype(F32),
        *gain_grads,
    )


def solution(mesh):
    rows = P(ROWS, None)
    cols = P(ROWS, "tensor")
    flipped = P("tensor", ROWS)
    vector = P(ROWS)
    return jax.shard_map(
        on_device,
        mesh=mesh,
        in_specs=(
            rows,
            P("dp", None),
            P("dp", None),
            cols,
            cols,
            cols,
            flipped,
            cols,
            cols,
            flipped,
            vector,
            vector,
            vector,
            vector,
            rows,
        ),
        out_specs=(
            rows,
            rows,
            cols,
            cols,
            cols,
            flipped,
            cols,
            cols,
            flipped,
            vector,
            vector,
            vector,
            vector,
        ),
        check_vma=False,
    )
```

profile of v0, /device:TPU:0, one launch (start us, length us, event | category | flops | bytes accessed | tf_op | source)
XLA Modules:
  0.0 778.3 jit_solution(5190589777838731769)
XLA Ops:
  13.0 33.2 %all-reduce = bf16[4352]{0:T(1024)(128)(2,1)S(1)} all-reduce(bf16[4352]{0:T(1024)(128)(2,1)S(1)} %dynamic-update-slice), channel_id=2, replica_groups=mesh['dp'=2,'ctx'=4,'tensor'=4] {'dp','ctx'}, use_global_device_ids=true, to_apply=%add | all-reduce | flops 4352 | bytes 17408
  90.7 27.2 %all-gather.10.cloned.1.call-done = bf16[2048,512]{1,0:T(8,128)(2,1)} async-done(((bf16[512,512]{1,0:T(8,128)(2,1)}), bf16[2048,512]{1,0:T(8,128)(2,1)}) %all-gather.10.cloned.1.call-update) | async-done | bytes 2097168 | tf_op jit(solution)/shard_map/all_gather | solution.py:203
  126.6 11.2 %fusion.127 = (f32[2,2,512]{2,1,0:T(2,128)S(1)}, f32[2,2,512,2048]{2,3,1,0:T(8,128)}) fusion(pred[512,2048]{0,1:T(8,128)(4,1)} %copy.47, bf16[2048,2,128,1]{0,2,3,1:T(8,128)(2,1)S(1)} %copy.71, bf16[512,2,2,64]{3,0,2,1:T(8,128)(2,1)} %bitcast.198, bf16[512,2,2,64]{3,0,2,1:T(8,128)(2,1)} %bitcast.196), kind=kOutput, calls=%fused_computation.254 | convolution fusion | flops 1091569664 | bytes 19406848 | tf_op jit(solution)/shard_map/sub | solution.py:214
  137.9 7.6 fusion.23
  157.5 9.4 %collective-permute-done = bf16[128,2048]{1,0:T(8,128)(2,1)S(1)} collective-permute-done((bf16[128,2048]{1,0:T(8,128)(2,1)S(1)}, bf16[128,2048]{1,0:T(8,128)(2,1)S(1)}, u32[]{:S(2)}, u32[]{:S(2)}) %collective-permute-start) | collective-permute-done | bytes 524320 | tf_op jit(solution)/shard_map/ppermute | solution.py:60
  166.8 11.5 %collective-permute-done.2 = bf16[128,2048]{1,0:T(8,128)(2,1)S(1)} collective-permute-done((bf16[128,2048]{1,0:T(8,128)(2,1)S(1)}, bf16[128,2048]{1,0:T(8,128)(2,1)S(1)}, u32[]{:S(2)}, u32[]{:S(2)}) %collective-permute-start.2) | collective-permute-done | bytes 524320 | tf_op jit(solution)/shard_map/ppermute | solution.py:60
  183.9 30.7 %all-gather.18.cloned.1.call-done = bf16[2048,1536]{0,1:T(8,128)(2,1)} async-done(((bf16[256,1536]{0,1:T(8,128)(2,1)}), bf16[2048,1536]{0,1:T(8,128)(2,1)}) %all-gather.18.cloned.1.call-update) | async-done | bytes 6291472 | tf_op jit(solution)/shard_map/all_gather | solution.py:153
  214.6 8.1 %fusion.112 = f32[512,1536]{1,0:T(8,128)} fusion(bf16[2048,1536]{0,1:T(8,128)(2,1)} %all-gather.18.cloned.1.call-done, bf16[128,2048]{1,0:T(8,128)(2,1)S(1)} %copy-done.42, bf16[128,2048]{1,0:T(8,128)(2,1)} %get-tuple-element.72, bf16[128,2048]{1,0:T(8,128)(2,1)S(1)} %copy-done.40, bf16[128,2048]{1,0:T(8,128)(2,1)S(1)} %copy-done.14), kind=kOutput, calls=%fused_computation.241 | convolution fusion | flops 3229614080 | bytes 11534336 | tf_op jit(solution)/shard_map/dot_general | solution.py:47
  222.7 56.2 %all-gather.16.cloned.1.call-done = bf16[2048,1536]{1,0:T(8,128)(2,1)} async-done(((bf16[256,1536]{1,0:T(8,128)(2,1)}), bf16[2048,1536]{1,0:T(8,128)(2,1)}) %all-gather.16.cloned.1.call-update) | async-done | bytes 6291472 | tf_op jit(solution)/shard_map/all_gather | solution.py:152
  279.0 8.5 %fusion.114 = f32[512,1536]{1,0:T(8,128)} fusion(bf16[2048,1536]{1,0:T(8,128)(2,1)} %all-gather.16.cloned.1.call-done, bf16[128,2048]{1,0:T(8,128)(2,1)} %collective-permute-done.5, bf16[128,2048]{1,0:T(8,128)(2,1)} %collective-permute-done.4, bf16[128,2048]{1,0:T(8,128)(2,1)} %collective-permute-done.3, bf16[128,2048]{1,0:T(8,128)(2,1)S(1)} %multiply_convert_fusion.4), kind=kOutput, calls=%fused_computation.243 | convolution fusion | flops 3229614080 | bytes 11534336 | tf_op jit(solution)/shard_map/dot_general | solution.py:47
  287.4 56.3 %all-gather.14.cloned.1.call-done = bf16[2048,1536]{1,0:T(8,128)(2,1)} async-done(((bf16[256,1536]{1,0:T(8,128)(2,1)}), bf16[2048,1536]{1,0:T(8,128)(2,1)}) %all-gather.14.cloned.1.call-update) | async-done | bytes 6291472 | tf_op jit(solution)/shard_map/all_gather | solution.py:151
  343.8 11.2 %multiply_convert_fusion.1 = (bf16[512,1536]{1,0:T(8,128)(2,1)S(1)}, bf16[512,1536]{1,0:T(8,128)(2,1)S(1)}, bf16[512,1536]{1,0:T(8,128)(2,1)}) fusion(f32[512,1536]{1,0:T(8,128)} %fusion.112, f32[512,1536]{1,0:T(8,128)} %fusion.114, bf16[2048,1536]{1,0:T(8,128)(2,1)} %all-gather.14.cloned.1.call-done, bf16[128,2048]{1,0:T(8,128)(2,1)} %collective-permute-done.5, ...), kind=kOutput, calls=%fused_computation.28 | convolution fusion | flops 3241410560 | bytes 19398656 | tf_op jit(solution)/shard_map/dot_general | solution.py:47
  369.0 11.3 %collective-permute-done.12 = bf16[128,2048]{1,0:T(8,128)(2,1)S(1)} collective-permute-done((bf16[128,2048]{1,0:T(8,128)(2,1)S(1)}, bf16[128,2048]{1,0:T(8,128)(2,1)S(1)}, u32[]{:S(2)}, u32[]{:S(2)}) %collective-permute-start.12) | collective-permute-done | bytes 524320 | tf_op jit(solution)/shard_map/ppermute | solution.py:60
  380.4 11.5 %collective-permute-done.14 = bf16[128,2048]{1,0:T(8,128)(2,1)S(1)} collective-permute-done((bf16[128,2048]{1,0:T(8,128)(2,1)S(1)}, bf16[128,2048]{1,0:T(8,128)(2,1)S(1)}, u32[]{:S(2)}, u32[]{:S(2)}) %collective-permute-start.14) | collective-permute-done | bytes 524320 | tf_op jit(solution)/shard_map/ppermute | solution.py:60
  397.8 12.2 %collective-permute-done.17 = bf16[128,2048]{1,0:T(8,128)(2,1)S(1)} collective-permute-done((bf16[128,2048]{1,0:T(8,128)(2,1)S(1)}, bf16[128,2048]{1,0:T(8,128)(2,1)S(1)}, u32[]{:S(2)}, u32[]{:S(2)}) %collective-permute-start.17) | collective-permute-done | bytes 524320 | tf_op jit(solution)/shard_map/ppermute | solution.py:60
  410.0 9.1 %collective-permute-done.16 = bf16[128,2048]{1,0:T(8,128)(2,1)S(1)} collective-permute-done((bf16[128,2048]{1,0:T(8,128)(2,1)S(1)}, bf16[128,2048]{1,0:T(8,128)(2,1)S(1)}, u32[]{:S(2)}, u32[]{:S(2)}) %collective-permute-start.16) | collective-permute-done | bytes 524320 | tf_op jit(solution)/shard_map/ppermute | solution.py:60
  420.4 9.7 %fusion.18 = bf16[2,128,2048]{2,1,0:T(8,128)(2,1)} fusion(bf16[512,2,2,128]{0,3,2,1:T(8,128)(2,1)S(1)} %bitcast.227, f32[2,2,512,2048]{2,3,1,0:T(8,128)} %get-tuple-element.115, f32[2,2,512]{2,1,0:T(2,128)S(1)} %get-tuple-element.114), kind=kOutput, calls=%fused_computation.38 | convolution fusion | flops 1082654720 | bytes 18358272 | tf_op jit(solution)/shard_map/kgts,tkgd->skd/dot_general | solution.py:252
  430.2 10.7 %fusion.1 = (f32[2,2,512]{2,1,0:T(2,128)S(1)}, f32[2,2048,512,2]{2,1,3,0:T(8,128)}) fusion(f32[2,2,512,2048]{2,3,1,0:T(8,128)} %get-tuple-element.115, f32[2,2,512]{2,1,0:T(2,128)S(1)} %get-tuple-element.114, bf16[512,2,2,128]{0,3,2,1:T(8,128)(2,1)S(1)} %bitcast.228, bf16[2048,2,128,1]{2,1,0,3:T(2,128)(2,1)S(1)} %bitcast.205), kind=kOutput, calls=%fused_computation.3 | convolution fusion | flops 1086322688 | bytes 35143680 | tf_op jit(solution)/shard_map/tkgd,skd->kgts/dot_general | solution.py:251
  443.1 12.1 %fusion.3 = bf16[2,2,512,2048]{2,3,1,0:T(8,128)(2,1)S(1)} fusion(f32[2,2048,512,2]{2,1,3,0:T(8,128)} %get-tuple-element.121, f32[2,2,512]{2,1,0:T(2,128)S(1)} %get-tuple-element.120, f32[2,2,512,2048]{2,3,1,0:T(8,128)} %get-tuple-element.115, f32[2,2,512]{2,1,0:T(2,128)S(1)} %get-tuple-element.114), kind=kLoop, calls=%fused_computation.5 | loop fusion | flops 16777216 | bytes 41959424 | tf_op jit(solution)/shard_map/convert_element_type | solution.py:254
  480.6 6.2 add_convert_fusion
  491.8 5.5 collective-permute-done.26
  506.5 5.8 collective-permute-done.27
  512.4 6.4 add_convert_fusion.1
  567.7 5.7 collective-permute-done.18
  573.9 10.8 %collective-permute-done.20 = bf16[128,2048]{1,0:T(8,128)(2,1)} collective-permute-done((bf16[128,2048]{1,0:T(8,128)(2,1)}, bf16[128,2048]{1,0:T(8,128)(2,1)}, u32[]{:S(2)}, u32[]{:S(2)}) %collective-permute-start.20) | collective-permute-done | bytes 524320 | tf_op jit(solution)/shard_map/ppermute | solution.py:60
  589.0 7.0 collective-permute-done.6
  596.0 10.4 %collective-permute-done.8 = bf16[128,2048]{1,0:T(8,128)(2,1)} collective-permute-done((bf16[128,2048]{1,0:T(8,128)(2,1)}, bf16[128,2048]{1,0:T(8,128)(2,1)}, u32[]{:S(2)}, u32[]{:S(2)}) %collective-permute-start.8) | collective-permute-done | bytes 524320 | tf_op jit(solution)/shard_map/ppermute | solution.py:60
  617.9 52.7 %psum.7 = f32[4352]{0:T(1024)S(1)} all-reduce(f32[4352]{0:T(1024)S(1)} %pad_maximum_fusion.15), channel_id=1, replica_groups=mesh['dp'=2,'ctx'=4,'tensor'=4] {'dp','ctx','tensor'}, use_global_device_ids=true, to_apply=%region_26.27 | all-reduce | flops 4352 | bytes 34816 | tf_op jit(solution)/shard_map/psum | solution.py:297
  677.1 10.7 %collective-permute-done.11 = bf16[128,2048]{1,0:T(8,128)(2,1)S(1)} collective-permute-done((bf16[128,2048]{1,0:T(8,128)(2,1)}, bf16[128,2048]{1,0:T(8,128)(2,1)S(1)}, u32[]{:S(2)}, u32[]{:S(2)}) %collective-permute-start.11) | collective-permute-done | bytes 524320 | tf_op jit(solution)/shard_map/ppermute | solution.py:60
  687.8 9.3 %collective-permute-done.10 = bf16[128,2048]{1,0:T(8,128)(2,1)S(1)} collective-permute-done((bf16[128,2048]{1,0:T(8,128)(2,1)}, bf16[128,2048]{1,0:T(8,128)(2,1)S(1)}, u32[]{:S(2)}, u32[]{:S(2)}) %collective-permute-start.10) | collective-permute-done | bytes 524320 | tf_op jit(solution)/shard_map/ppermute | solution.py:60
  707.2 14.8 %reduce-scatter.15.cloned.1.call-done = bf16[256,1536]{1,0:T(8,128)(2,1)} async-done(((bf16[1024,1536]{1,0:T(8,128)(2,1)}), bf16[256,1536]{1,0:T(8,128)(2,1)}) %reduce-scatter.15.cloned.1.call-update) | async-done | bytes 786448 | tf_op jit(solution)/shard_map/reduce_scatter | solution.py:98
  724.4 43.3 %reduce-scatter.9.cloned.1.call-done = bf16[256,1024]{1,0:T(8,128)(2,1)} async-done(((bf16[1024,1024]{1,0:T(8,128)(2,1)}), bf16[256,1024]{1,0:T(8,128)(2,1)}) %reduce-scatter.9.cloned.1.call-update) | async-done | bytes 524304 | tf_op jit(solution)/shard_map/reduce_scatter | solution.py:98
  (360 shorter events, 225.7 us)
Async XLA Ops:
  7.2 53.6 %all-gather.8.cloned.1.call-start = ((), (), s32[]{:S(2)}) async-start(), calls=%async_computation.6 | async-start | bytes 4718592 | tf_op jit(solution)/shard_map/all_gather | solution.py:147
  9.2 108.7 %all-gather.10.cloned.1.call-start = ((), (), s32[]{:S(2)}) async-start(), calls=%async_computation.7 | async-start | bytes 2621440 | tf_op jit(solution)/shard_map/all_gather | solution.py:203
  73.2 75.7 %all-gather.12.cloned.1.call-start = ((), (), s32[]{:S(2)}) async-start(), calls=%async_computation.8 | async-start | bytes 2359296 | tf_op jit(solution)/shard_map/all_gather | solution.py:150
  74.0 140.6 %all-gather.18.cloned.1.call-start = ((), (), s32[]{:S(2)}) async-start(), calls=%async_computation.11 | async-start | bytes 7077888 | tf_op jit(solution)/shard_map/all_gather | solution.py:153
  74.5 204.4 %all-gather.16.cloned.1.call-start = ((), (), s32[]{:S(2)}) async-start(), calls=%async_computation.10 | async-start | bytes 7077888 | tf_op jit(solution)/shard_map/all_gather | solution.py:152
  75.1 268.7 %all-gather.14.cloned.1.call-start = ((), (), s32[]{:S(2)}) async-start(), calls=%async_computation.9 | async-start | bytes 7077888 | tf_op jit(solution)/shard_map/all_gather | solution.py:151
  75.7 459.8 %reduce-scatter.7.cloned.1.call-start = ((), (), s32[]{:S(2)}) async-start(), calls=%async_computation.12 | async-start | bytes 2621440 | tf_op jit(solution)/shard_map/reduce_scatter | solution.py:262
  153.4 24.8 %collective-permute-start.2 = (bf16[128,2048]{1,0:T(8,128)(2,1)S(1)}, bf16[128,2048]{1,0:T(8,128)(2,1)S(1)}, u32[]{:S(2)}, u32[]{:S(2)}) collective-permute-start(bf16[128,2048]{1,0:T(8,128)(2,1)S(1)} %get-tuple-element.81), channel_id=1, source_target_pairs={{0,3},{1,2},{2,1},{3,0},{4,7},{5,6},{6,5},{7,4},{8,11},{9,10},{10,... | collective-permute-start | bytes 1572872 | tf_op jit(solution)/shard_map/ppermute | solution.py:60
  154.9 24.7 %collective-permute-start.1 = (bf16[128,2048]{1,0:T(8,128)(2,1)S(1)}, bf16[128,2048]{1,0:T(8,128)(2,1)S(1)}, u32[]{:S(2)}, u32[]{:S(2)}) collective-permute-start(bf16[128,2048]{1,0:T(8,128)(2,1)S(1)} %get-tuple-element.82), channel_id=1, source_target_pairs={{0,2},{1,3},{2,0},{3,1},{4,6},{5,7},{6,4},{7,5},{8,10},{9,11},{10,... | collective-permute-start | bytes 1572872 | tf_op jit(solution)/shard_map/ppermute | solution.py:60
  180.3 98.7 %collective-permute-start.5 = (bf16[128,2048]{1,0:T(8,128)(2,1)S(1)}, bf16[128,2048]{1,0:T(8,128)(2,1)}, u32[]{:S(2)}, u32[]{:S(2)}) collective-permute-start(bf16[128,2048]{1,0:T(8,128)(2,1)S(1)} %multiply_convert_fusion.4), channel_id=1, source_target_pairs={{0,3},{1,2},{2,1},{3,0},{4,7},{5,6},{6,5},{7,4},{8,11},{9,10},{10,... | collective-permute-start | bytes 1572872 | tf_op jit(solution)/shard_map/ppermute | solution.py:60
  181.8 97.1 %collective-permute-start.4 = (bf16[128,2048]{1,0:T(8,128)(2,1)S(1)}, bf16[128,2048]{1,0:T(8,128)(2,1)}, u32[]{:S(2)}, u32[]{:S(2)}) collective-permute-start(bf16[128,2048]{1,0:T(8,128)(2,1)S(1)} %multiply_convert_fusion.4), channel_id=1, source_target_pairs={{0,2},{1,3},{2,0},{3,1},{4,6},{5,7},{6,4},{7,5},{8,10},{9,11},{10,... | collective-permute-start | bytes 1572872 | tf_op jit(solution)/shard_map/ppermute | solution.py:60
  183.3 95.7 %collective-permute-start.3 = (bf16[128,2048]{1,0:T(8,128)(2,1)S(1)}, bf16[128,2048]{1,0:T(8,128)(2,1)}, u32[]{:S(2)}, u32[]{:S(2)}) collective-permute-start(bf16[128,2048]{1,0:T(8,128)(2,1)S(1)} %multiply_convert_fusion.4), channel_id=1, source_target_pairs={{0,1},{1,0},{2,3},{3,2},{4,5},{5,4},{6,7},{7,6},{8,9},{9,8},{10,11... | collective-permute-start | bytes 1572872 | tf_op jit(solution)/shard_map/ppermute | solution.py:60
  367.0 24.8 %collective-permute-start.14 = (bf16[128,2048]{1,0:T(8,128)(2,1)S(1)}, bf16[128,2048]{1,0:T(8,128)(2,1)S(1)}, u32[]{:S(2)}, u32[]{:S(2)}) collective-permute-start(bf16[128,2048]{1,0:T(8,128)(2,1)S(1)} %get-tuple-element.67), channel_id=1, source_target_pairs={{0,3},{1,2},{2,1},{3,0},{4,7},{5,6},{6,5},{7,4},{8,11},{9,10},{10,... | collective-permute-start | bytes 1572872 | tf_op jit(solution)/shard_map/ppermute | solution.py:60
  368.5 24.7 %collective-permute-start.13 = (bf16[128,2048]{1,0:T(8,128)(2,1)S(1)}, bf16[128,2048]{1,0:T(8,128)(2,1)S(1)}, u32[]{:S(2)}, u32[]{:S(2)}) collective-permute-start(bf16[128,2048]{1,0:T(8,128)(2,1)S(1)} %get-tuple-element.68), channel_id=1, source_target_pairs={{0,2},{1,3},{2,0},{3,1},{4,6},{5,7},{6,4},{7,5},{8,10},{9,11},{10,... | collective-permute-start | bytes 1572872 | tf_op jit(solution)/shard_map/ppermute | solution.py:60
  395.8 23.3 %collective-permute-start.16 = (bf16[128,2048]{1,0:T(8,128)(2,1)S(1)}, bf16[128,2048]{1,0:T(8,128)(2,1)S(1)}, u32[]{:S(2)}, u32[]{:S(2)}) collective-permute-start(bf16[128,2048]{1,0:T(8,128)(2,1)S(1)} %fusion.111), channel_id=1, source_target_pairs={{0,2},{1,3},{2,0},{3,1},{4,6},{5,7},{6,4},{7,5},{8,10},{9,11},{10,... | collective-permute-start | bytes 1572872 | tf_op jit(solution)/shard_map/ppermute | solution.py:60
  397.2 21.8 %collective-permute-start.15 = (bf16[128,2048]{1,0:T(8,128)(2,1)S(1)}, bf16[128,2048]{1,0:T(8,128)(2,1)S(1)}, u32[]{:S(2)}, u32[]{:S(2)}) collective-permute-start(bf16[128,2048]{1,0:T(8,128)(2,1)S(1)} %fusion.111), channel_id=1, source_target_pairs={{0,1},{1,0},{2,3},{3,2},{4,5},{5,4},{6,7},{7,6},{8,9},{9,8},{10,11... | collective-permute-start | bytes 1572872 | tf_op jit(solution)/shard_map/ppermute | solution.py:60
  464.3 151.6 %reduce-scatter.11.cloned.1.call-start = ((), (), s32[]{:S(2)}) async-start(), calls=%async_computation.14 | async-start | bytes 1310720 | tf_op jit(solution)/shard_map/reduce_scatter | solution.py:98
  480.6 221.2 %reduce-scatter.17.cloned.1.call-start = ((), (), s32[]{:S(2)}) async-start(), calls=%async_computation.17 | async-start | bytes 3932160 | tf_op jit(solution)/shard_map/reduce_scatter | solution.py:98
  486.9 217.8 %reduce-scatter.13.cloned.1.call-start = ((), (), s32[]{:S(2)}) async-start(), calls=%async_computation.15 | async-start | bytes 3932160 | tf_op jit(solution)/shard_map/reduce_scatter | solution.py:98
  500.9 221.0 %reduce-scatter.15.cloned.1.call-start = ((), (), s32[]{:S(2)}) async-start(), calls=%async_computation.16 | async-start | bytes 3932160 | tf_op jit(solution)/shard_map/reduce_scatter | solution.py:98
  518.8 248.9 %reduce-scatter.9.cloned.1.call-start = ((), (), s32[]{:S(2)}) async-start(), calls=%async_computation.13 | async-start | bytes 2621440 | tf_op jit(solution)/shard_map/reduce_scatter | solution.py:98
  545.8 18.0 %collective-permute-start.24 = (bf16[1024,1024]{1,0:T(8,128)(2,1)S(1)}, bf16[1024,1024]{1,0:T(8,128)(2,1)S(1)}, u32[]{:S(2)}, u32[]{:S(2)}) collective-permute-start(bf16[1024,1024]{1,0:T(8,128)(2,1)S(1)} %convolution_convert_fusion.3), channel_id=1, source_target_pairs={{0,16},{16,0},{1,17},{17,1},{2,18},{18,2},{3,19},{19,3},{4,20},{20... | collective-permute-start | bytes 6291464 | tf_op jit(solution)/shard_map/ppermute | solution.py:60
  559.1 25.5 %collective-permute-start.20 = (bf16[128,2048]{1,0:T(8,128)(2,1)}, bf16[128,2048]{1,0:T(8,128)(2,1)}, u32[]{:S(2)}, u32[]{:S(2)}) collective-permute-start(bf16[128,2048]{1,0:T(8,128)(2,1)} %get-tuple-element.64), channel_id=1, source_target_pairs={{0,3},{1,2},{2,1},{3,0},{4,7},{5,6},{6,5},{7,4},{8,11},{9,10},{10,... | collective-permute-start | bytes 1572872 | tf_op jit(solution)/shard_map/ppermute | solution.py:60
  560.3 26.3 %collective-permute-start.19 = (bf16[128,2048]{1,0:T(8,128)(2,1)}, bf16[128,2048]{1,0:T(8,128)(2,1)}, u32[]{:S(2)}, u32[]{:S(2)}) collective-permute-start(bf16[128,2048]{1,0:T(8,128)(2,1)} %get-tuple-element.65), channel_id=1, source_target_pairs={{0,2},{1,3},{2,0},{3,1},{4,6},{5,7},{6,4},{7,5},{8,10},{9,11},{10,... | collective-permute-start | bytes 1572872 | tf_op jit(solution)/shard_map/ppermute | solution.py:60
  563.0 33.0 %collective-permute-start.6 = (bf16[128,2048]{1,0:T(8,128)(2,1)}, bf16[128,2048]{1,0:T(8,128)(2,1)}, u32[]{:S(2)}, u32[]{:S(2)}) collective-permute-start(bf16[128,2048]{1,0:T(8,128)(2,1)} %get-tuple-element.77), channel_id=1, source_target_pairs={{0,1},{1,0},{2,3},{3,2},{4,5},{5,4},{6,7},{7,6},{8,9},{9,8},{10,11... | collective-permute-start | bytes 1572872 | tf_op jit(solution)/shard_map/ppermute | solution.py:60
  563.8 42.6 %collective-permute-start.8 = (bf16[128,2048]{1,0:T(8,128)(2,1)}, bf16[128,2048]{1,0:T(8,128)(2,1)}, u32[]{:S(2)}, u32[]{:S(2)}) collective-permute-start(bf16[128,2048]{1,0:T(8,128)(2,1)} %get-tuple-element.78), channel_id=1, source_target_pairs={{0,3},{1,2},{2,1},{3,0},{4,7},{5,6},{6,5},{7,4},{8,11},{9,10},{10,... | collective-permute-start | bytes 1572872 | tf_op jit(solution)/shard_map/ppermute | solution.py:60
  573.4 34.3 %collective-permute-start.7 = (bf16[128,2048]{1,0:T(8,128)(2,1)}, bf16[128,2048]{1,0:T(8,128)(2,1)S(1)}, u32[]{:S(2)}, u32[]{:S(2)}) collective-permute-start(bf16[128,2048]{1,0:T(8,128)(2,1)} %get-tuple-element.79), channel_id=1, source_target_pairs={{0,2},{1,3},{2,0},{3,1},{4,6},{5,7},{6,4},{7,5},{8,10},{9,11},{10,... | collective-permute-start | bytes 1572872 | tf_op jit(solution)/shard_map/ppermute | solution.py:60
  612.4 63.2 %collective-permute-start.23 = (bf16[128,2048]{1,0:T(8,128)(2,1)}, bf16[128,2048]{1,0:T(8,128)(2,1)S(1)}, u32[]{:S(2)}, u32[]{:S(2)}) collective-permute-start(bf16[128,2048]{1,0:T(8,128)(2,1)} %get-tuple-element.91), channel_id=1, source_target_pairs={{0,3},{1,2},{2,1},{3,0},{4,7},{5,6},{6,5},{7,4},{8,11},{9,10},{10,... | collective-permute-start | bytes 1572872 | tf_op jit(solution)/shard_map/ppermute | solution.py:60
  614.2 61.5 %collective-permute-start.22 = (bf16[128,2048]{1,0:T(8,128)(2,1)}, bf16[128,2048]{1,0:T(8,128)(2,1)S(1)}, u32[]{:S(2)}, u32[]{:S(2)}) collective-permute-start(bf16[128,2048]{1,0:T(8,128)(2,1)} %get-tuple-element.91), channel_id=1, source_target_pairs={{0,2},{1,3},{2,0},{3,1},{4,6},{5,7},{6,4},{7,5},{8,10},{9,11},{10,... | collective-permute-start | bytes 1572872 | tf_op jit(solution)/shard_map/ppermute | solution.py:60
  615.3 60.3 %collective-permute-start.21 = (bf16[128,2048]{1,0:T(8,128)(2,1)}, bf16[128,2048]{1,0:T(8,128)(2,1)S(1)}, u32[]{:S(2)}, u32[]{:S(2)}) collective-permute-start(bf16[128,2048]{1,0:T(8,128)(2,1)} %get-tuple-element.91), channel_id=1, source_target_pairs={{0,1},{1,0},{2,3},{3,2},{4,5},{5,4},{6,7},{7,6},{8,9},{9,8},{10,11... | collective-permute-start | bytes 1572872 | tf_op jit(solution)/shard_map/ppermute | solution.py:60
  674.2 22.9 %collective-permute-start.10 = (bf16[128,2048]{1,0:T(8,128)(2,1)}, bf16[128,2048]{1,0:T(8,128)(2,1)S(1)}, u32[]{:S(2)}, u32[]{:S(2)}) collective-permute-start(bf16[128,2048]{1,0:T(8,128)(2,1)} %get-tuple-element.92), channel_id=1, source_target_pairs={{0,2},{1,3},{2,0},{3,1},{4,6},{5,7},{6,4},{7,5},{8,10},{9,11},{10,... | collective-permute-start | bytes 1572872 | tf_op jit(solution)/shard_map/ppermute | solution.py:60
  675.6 21.5 %collective-permute-start.9 = (bf16[128,2048]{1,0:T(8,128)(2,1)}, bf16[128,2048]{1,0:T(8,128)(2,1)S(1)}, u32[]{:S(2)}, u32[]{:S(2)}) collective-permute-start(bf16[128,2048]{1,0:T(8,128)(2,1)} %get-tuple-element.92), channel_id=1, source_target_pairs={{0,1},{1,0},{2,3},{3,2},{4,5},{5,4},{6,7},{7,6},{8,9},{9,8},{10,11... | collective-permute-start | bytes 1572872 | tf_op jit(solution)/shard_map/ppermute | solution.py:60
  (83 other events, 1321.9 us)
Sparse Core Ops, SparseCore 0:
  10.2 50.5 all-gather.7
  73.3 44.5 all-gather.9
  119.5 29.4 all-gather.11
  150.4 64.1 all-gather.17
  216.0 62.8 all-gather.15
  280.4 63.3 all-gather.13
  464.4 41.3 reduce-scatter.6
  508.2 26.4 reduce-scatter.10
  537.0 58.9 reduce-scatter.16
  598.1 61.0 reduce-scatter.12
  661.5 60.4 reduce-scatter.14
  724.1 43.5 reduce-scatter.8
where the time goes:
time: 786 us; the launch traced here: 778 us
  waiting for transfers between devices  376 us (48%)
  matrix products  147 us (19%)
  blocking collectives  86 us (11%)
  other arithmetic  73.9 us (9%)
  local copies, waits for them, and re-layouts  49.5 us (6%)
  starting transfers between devices  29.6 us (4%)
  between operations  16.3 us (2%)
    ppermute x29, waiting for transfers between devices, swap(): return lax.ppermute(values, axis, [(a, a ^ mask) for a in range(size)])  140 us
    reduce_scatter x5, waiting for transfers between devices, grad_scatter(): return lax.psum_scatter(both, 'ctx', scatter_dimension=0, tiled=True)  58 us
    all_gather x1, waiting for transfers between devices, on_device(): wg_full = lax.all_gather(w_gate, ROWS, axis=0, tiled=True)  56.3 us
    all_gather x1, waiting for transfers between devices, on_device(): wu_full = lax.all_gather(w_up, ROWS, axis=0, tiled=True)  56.2 us
    psum x1, blocking collectives, on_device(): lax.psum(jnp.concatenate([gain_one_part, gain_two_part, jnp.sum(q_gain_te...  52.7 us
    dot_general x10, matrix products, inner_rows(): lax.dot_general(left, right, (((0,), (0,)), ((), ())), preferred_element_...  35.8 us
    dot_general x5, matrix products, dot(): return jnp.dot(left, right, preferred_element_type=F32)  34.2 us
    unnamed x1, blocking collectives  33.2 us
  transfers between devices with their start and end apart: 41, of which 27 were waited for; matrix products, arithmetic and copies ran while one was open for 23% of the time, Pallas kernels for 0%

commit v1 on v0

--- a/solution.py
+++ b/solution.py
@@ -11,6 +11,12 @@
 BF = jnp.bfloat16
 F32 = jnp.float32
 ROWS = ("dp", "ctx")
+
+
+def in_order(blocks, dim):
+    blocks = jnp.moveaxis(blocks, 0, dim)
+    shape = blocks.shape
+    return blocks.reshape(*shape[:dim], shape[dim] * shape[dim + 1], *shape[dim + 2 :])
 
 
 def row_scales(values):
@@ -148,7 +154,19 @@
         jnp.concatenate([w_query, w_key, w_value], axis=1), ROWS, axis=0, tiled=True
     )
     wo_t = lax.all_gather(w_out.T, ROWS, axis=0, tiled=True)
-    wg_full = lax.all_gather(w_gate, ROWS, axis=0, tiled=True)
+    count = lax.axis_size(ROWS)
+    pairs = [(i, (i + 1) % count) for i in range(count)]
+    back = [(b, a_2) for a_2, b in pairs]
+    lower, upper = ([], [])
+    for step in range(count - 1):
+        if step % 2 == 0:
+            lower.append(lax.ppermute(lower[-1] if lower else w_gate, ROWS, pairs))
+        else:
+            upper.append(lax.ppermute(upper[-1] if upper else w_gate, ROWS, back))
+    blocks = jnp.stack([*lower[::-1], w_gate, *upper])
+    shift = lax.axis_index(ROWS) - len(lower)
+    blocks = blocks[(jnp.arange(count) - shift) % count]
+    wg_full = in_order(blocks, 0)
     wu_full = lax.all_gather(w_up, ROWS, axis=0, tiled=True)
     wd_t = lax.all_gather(w_down.T, ROWS, axis=0, tiled=True)
     gain_sizes = (gain_attn.shape[0], gain_mlp.shape[0], gain_query.shape[0], gain_key.shape[0])

time: 786 us -> 812 us (1.033)
  local copies, waits for them, and re-layouts: 49.5 us -> 63.6 us
  starting transfers between devices: 29.6 us -> 42.5 us
    ppermute x0 -> x7, waiting for transfers between devices: none -> 131 us  [the longest x4 103 us: on_device(): lower.append(lax.ppermute(lower[-1] if lower else w_gate, ROWS, pairs))]
    all_gather x1 -> x0, waiting for transfers between devices: 56.3 us -> none  [on_device(): wg_full = lax.all_gather(w_gate, ROWS, axis=0, tiled=True)]
    all_gather x1, waiting for transfers between devices: 30.7 us -> 0.01 us  [on_device(): wd_t = lax.all_gather(w_down.T, ROWS, axis=0, tiled=True)]
    all_gather x1, waiting for transfers between devices: 27.2 us -> 0.01 us  [on_device(): lax.all_gather(jnp.concatenate([k_bf.reshape(row_count, k_cols), v_bf], a...]
    ppermute x0 -> x7, starting transfers between devices: none -> 12.2 us  [the longest x4 11.7 us: on_device(): lower.append(lax.ppermute(lower[-1] if lower else w_gate, ROWS, pairs))]
    ppermute x29, waiting for transfers between devices: 140 us -> 129 us  [swap(): return lax.ppermute(values, axis, [(a, a ^ mask) for a in range(size)])]
    unnamed x158 -> x183, local copies, waits for them, and re-layouts: 14.5 us -> 23.9 us
  transfers between devices with their start and end apart: 41 -> 47, of which waited for: 27 -> 29; matrix products, arithmetic and copies ran while one was open for 23% -> 24% of each run, Pallas kernels for 0% -> 0%
where the time goes in v1:
time: 812 us; the launch traced here: 803 us
  waiting for transfers between devices  375 us (46%)
  matrix products  143 us (18%)
  blocking collectives  86.4 us (11%)
  other arithmetic  76.5 us (9%)
  local copies, waits for them, and re-layouts  63.6 us (8%)
  starting transfers between devices  42.5 us (5%)
  between operations  16.2 us (2%)
    ppermute x29, waiting for transfers between devices, swap(): return lax.ppermute(values, axis, [(a, a ^ mask) for a in range(size)])  129 us
    ppermute x4, waiting for transfers between devices, on_device(): lower.append(lax.ppermute(lower[-1] if lower else w_gate, ROWS, pairs))  103 us
    reduce_scatter x5, waiting for transfers between devices, grad_scatter(): return lax.psum_scatter(both, 'ctx', scatter_dimension=0, tiled=True)  58 us
    all_gather x1, waiting for transfers between devices, on_device(): wu_full = lax.all_gather(w_up, ROWS, axis=0, tiled=True)  53.5 us
    psum x1, blocking collectives, on_device(): lax.psum(jnp.concatenate([gain_one_part, gain_two_part, jnp.sum(q_gain_te...  53.2 us
    dot_general x10, matrix products, inner_rows(): lax.dot_general(left, right, (((0,), (0,)), ((), ())), preferred_element_...  36 us
    unnamed x1, blocking collectives  33.2 us
    dot_general x5, matrix products, dot(): return jnp.dot(left, right, preferred_element_type=F32)  30.3 us
  transfers between devices with their start and end apart: 47, of which 29 were waited for; matrix products, arithmetic and copies ran while one was open for 24% of the time, Pallas kernels for 0%

profile of v1, /device:TPU:0, one launch (start us, length us, event | category | flops | bytes accessed | tf_op | source)
XLA Modules:
  0.0 803.2 jit_solution(10005455635735425830)
XLA Ops:
  13.0 33.2 %all-reduce = bf16[4352]{0:T(1024)(128)(2,1)S(1)} all-reduce(bf16[4352]{0:T(1024)(128)(2,1)S(1)} %dynamic-update-slice), channel_id=2, replica_groups=mesh['dp'=2,'ctx'=4,'tensor'=4] {'dp','ctx'}, use_global_device_ids=true, to_apply=%add | all-reduce | flops 4352 | bytes 17408
  74.8 33.0 %collective-permute-done.6 = bf16[256,1536]{1,0:T(8,128)(2,1)} collective-permute-done((bf16[256,1536]{1,0:T(8,128)(2,1)}, bf16[256,1536]{1,0:T(8,128)(2,1)}, u32[]{:S(2)}, u32[]{:S(2)}) %collective-permute-start.6) | collective-permute-done | bytes 786464 | tf_op jit(solution)/shard_map/ppermute | solution.py:163
  107.8 10.3 %collective-permute-start.7 = (bf16[256,1536]{1,0:T(8,128)(2,1)}, bf16[256,1536]{1,0:T(8,128)(2,1)}, u32[]{:S(2)}, u32[]{:S(2)}) collective-permute-start(bf16[256,1536]{1,0:T(8,128)(2,1)} %collective-permute-done.6), channel_id=1, source_target_pairs={{0,4},{4,8},{8,12},{12,16},{16,20},{20,24},{24,28},{28,0},{1,5},{5... | collective-permute-start | bytes 2359304 | tf_op jit(solution)/shard_map/ppermute | solution.py:163
  118.4 27.8 %collective-permute-done.7 = bf16[256,1536]{1,0:T(8,128)(2,1)} collective-permute-done((bf16[256,1536]{1,0:T(8,128)(2,1)}, bf16[256,1536]{1,0:T(8,128)(2,1)}, u32[]{:S(2)}, u32[]{:S(2)}) %collective-permute-start.7) | collective-permute-done | bytes 786464 | tf_op jit(solution)/shard_map/ppermute | solution.py:163
  155.1 12.8 %collective-permute-done.10 = bf16[256,1536]{1,0:T(8,128)(2,1)} collective-permute-done((bf16[256,1536]{1,0:T(8,128)(2,1)}, bf16[256,1536]{1,0:T(8,128)(2,1)}, u32[]{:S(2)}, u32[]{:S(2)}) %collective-permute-start.10) | collective-permute-done | bytes 786464 | tf_op jit(solution)/shard_map/ppermute | solution.py:165
  167.9 26.9 %collective-permute-done.8 = bf16[256,1536]{1,0:T(8,128)(2,1)} collective-permute-done((bf16[256,1536]{1,0:T(8,128)(2,1)}, bf16[256,1536]{1,0:T(8,128)(2,1)}, u32[]{:S(2)}, u32[]{:S(2)}) %collective-permute-start.8) | collective-permute-done | bytes 786464 | tf_op jit(solution)/shard_map/ppermute | solution.py:163
  200.2 15.3 %collective-permute-done.11 = bf16[256,1536]{1,0:T(8,128)(2,1)} collective-permute-done((bf16[256,1536]{1,0:T(8,128)(2,1)}, bf16[256,1536]{1,0:T(8,128)(2,1)}, u32[]{:S(2)}, u32[]{:S(2)}) %collective-permute-start.11) | collective-permute-done | bytes 786464 | tf_op jit(solution)/shard_map/ppermute | solution.py:165
  216.0 15.5 %collective-permute-done.9 = bf16[256,1536]{1,0:T(8,128)(2,1)S(1)} collective-permute-done((bf16[256,1536]{1,0:T(8,128)(2,1)}, bf16[256,1536]{1,0:T(8,128)(2,1)S(1)}, u32[]{:S(2)}, u32[]{:S(2)}) %collective-permute-start.9) | collective-permute-done | bytes 786464 | tf_op jit(solution)/shard_map/ppermute | solution.py:163
  248.3 11.5 %fusion.129 = (f32[2,2,512]{2,1,0:T(2,128)S(1)}, f32[2,2,512,2048]{2,3,1,0:T(8,128)}) fusion(pred[512,2048]{0,1:T(8,128)(4,1)} %copy.47, bf16[2048,2,128,1]{0,2,3,1:T(8,128)(2,1)S(1)} %copy.71, bf16[512,2,2,64]{3,0,2,1:T(8,128)(2,1)} %bitcast.221, bf16[512,2,2,64]{3,0,2,1:T(8,128)(2,1)S(1)} %bitcast.219), kind=kOutput, calls=%fused_computation.270 | convolution fusion | flops 1091569664 | bytes 19406848 | tf_op jit(solution)/shard_map/sub | solution.py:232
  259.8 7.2 fusion.23
  281.0 6.4 gather_fusion
  287.5 9.2 %collective-permute-done.2 = bf16[128,2048]{1,0:T(8,128)(2,1)S(1)} collective-permute-done((bf16[128,2048]{1,0:T(8,128)(2,1)}, bf16[128,2048]{1,0:T(8,128)(2,1)S(1)}, u32[]{:S(2)}, u32[]{:S(2)}) %collective-permute-start.2) | collective-permute-done | bytes 524320 | tf_op jit(solution)/shard_map/ppermute | solution.py:66
  306.3 8.2 %fusion.114 = f32[512,1536]{1,0:T(8,128)} fusion(bf16[2048,1536]{0,1:T(8,128)(2,1)} %all-gather.15.cloned.1.call-done, bf16[128,2048]{1,0:T(8,128)(2,1)S(1)} %copy-done.44, bf16[128,2048]{1,0:T(8,128)(2,1)} %get-tuple-element.72, bf16[128,2048]{1,0:T(8,128)(2,1)S(1)} %copy-done.42, bf16[128,2048]{1,0:T(8,128)(2,1)S(1)} %get-tuple-element.69), kind=kOutput, calls=%fused_computation.257 | convolution fusion | flops 3229614080 | bytes 11534336 | tf_op jit(solution)/shard_map/dot_general | solution.py:53
  314.5 53.5 %all-gather.13.cloned.1.call-done = bf16[2048,1536]{1,0:T(8,128)(2,1)} async-done(((bf16[256,1536]{1,0:T(8,128)(2,1)}), bf16[2048,1536]{1,0:T(8,128)(2,1)}) %all-gather.13.cloned.1.call-update) | async-done | bytes 6291472 | tf_op jit(solution)/shard_map/all_gather | solution.py:170
  368.0 6.5 fusion.116
  374.6 9.2 %multiply_convert_fusion.2 = (bf16[512,1536]{1,0:T(8,128)(2,1)S(1)}, bf16[512,1536]{1,0:T(8,128)(2,1)S(1)}, bf16[512,1536]{1,0:T(8,128)(2,1)}) fusion(f32[512,1536]{1,0:T(8,128)S(1)} %copy-done.75, f32[512,1536]{1,0:T(8,128)S(1)} %fusion.116, bf16[2048,1536]{1,0:T(8,128)(2,1)} %bitcast.209, bf16[128,2048]{1,0:T(8,128)(2,1)} %collective-permute-done.5, ...), kind=kOutput, calls=%fused_computation.30 | convolution fusion | flops 3241410560 | bytes 19398656 | tf_op jit(solution)/shard_map/dot_general | solution.py:53
  394.4 11.3 %collective-permute-done.19 = bf16[128,2048]{1,0:T(8,128)(2,1)S(1)} collective-permute-done((bf16[128,2048]{1,0:T(8,128)(2,1)S(1)}, bf16[128,2048]{1,0:T(8,128)(2,1)S(1)}, u32[]{:S(2)}, u32[]{:S(2)}) %collective-permute-start.19) | collective-permute-done | bytes 524320 | tf_op jit(solution)/shard_map/ppermute | solution.py:66
  405.7 11.5 %collective-permute-done.21 = bf16[128,2048]{1,0:T(8,128)(2,1)S(1)} collective-permute-done((bf16[128,2048]{1,0:T(8,128)(2,1)S(1)}, bf16[128,2048]{1,0:T(8,128)(2,1)S(1)}, u32[]{:S(2)}, u32[]{:S(2)}) %collective-permute-start.21) | collective-permute-done | bytes 524320 | tf_op jit(solution)/shard_map/ppermute | solution.py:66
  423.2 12.2 %collective-permute-done.24 = bf16[128,2048]{1,0:T(8,128)(2,1)S(1)} collective-permute-done((bf16[128,2048]{1,0:T(8,128)(2,1)S(1)}, bf16[128,2048]{1,0:T(8,128)(2,1)S(1)}, u32[]{:S(2)}, u32[]{:S(2)}) %collective-permute-start.24) | collective-permute-done | bytes 524320 | tf_op jit(solution)/shard_map/ppermute | solution.py:66
  435.4 9.1 %collective-permute-done.23 = bf16[128,2048]{1,0:T(8,128)(2,1)S(1)} collective-permute-done((bf16[128,2048]{1,0:T(8,128)(2,1)S(1)}, bf16[128,2048]{1,0:T(8,128)(2,1)S(1)}, u32[]{:S(2)}, u32[]{:S(2)}) %collective-permute-start.23) | collective-permute-done | bytes 524320 | tf_op jit(solution)/shard_map/ppermute | solution.py:66
  445.8 9.9 %fusion.18 = bf16[2,128,2048]{2,1,0:T(8,128)(2,1)} fusion(bf16[512,2,2,128]{0,3,2,1:T(8,128)(2,1)S(1)} %bitcast.252, f32[2,2,512,2048]{2,3,1,0:T(8,128)} %get-tuple-element.115, f32[2,2,512]{2,1,0:T(2,128)S(1)} %get-tuple-element.114), kind=kOutput, calls=%fused_computation.39 | convolution fusion | flops 1082654720 | bytes 18358272 | tf_op jit(solution)/shard_map/kgts,tkgd->skd/dot_general | solution.py:270
  455.7 10.6 %fusion.1 = (f32[2,2,512]{2,1,0:T(2,128)S(1)}, f32[2,2048,512,2]{2,1,3,0:T(8,128)}) fusion(f32[2,2,512,2048]{2,3,1,0:T(8,128)} %get-tuple-element.115, f32[2,2,512]{2,1,0:T(2,128)S(1)} %get-tuple-element.114, bf16[512,2,2,128]{0,3,2,1:T(8,128)(2,1)S(1)} %bitcast.253, bf16[2048,2,128,1]{2,1,0,3:T(2,128)(2,1)S(1)} %bitcast.228), kind=kOutput, calls=%fused_computation.4 | convolution fusion | flops 1086322688 | bytes 35143680 | tf_op jit(solution)/shard_map/tkgd,skd->kgts/dot_general | solution.py:269
  468.6 11.8 %fusion.3 = bf16[2,2,512,2048]{2,3,1,0:T(8,128)(2,1)S(1)} fusion(f32[2,2048,512,2]{2,1,3,0:T(8,128)} %get-tuple-element.121, f32[2,2,512]{2,1,0:T(2,128)S(1)} %get-tuple-element.120, f32[2,2,512,2048]{2,3,1,0:T(8,128)} %get-tuple-element.115, f32[2,2,512]{2,1,0:T(2,128)S(1)} %get-tuple-element.114), kind=kLoop, calls=%fused_computation.6 | loop fusion | flops 16777216 | bytes 41959424 | tf_op jit(solution)/shard_map/convert_element_type | solution.py:272
  536.7 6.4 add_convert_fusion.2
  598.7 10.8 %collective-permute-done.27 = bf16[128,2048]{1,0:T(8,128)(2,1)} collective-permute-done((bf16[128,2048]{1,0:T(8,128)(2,1)}, bf16[128,2048]{1,0:T(8,128)(2,1)}, u32[]{:S(2)}, u32[]{:S(2)}) %collective-permute-start.27) | collective-permute-done | bytes 524320 | tf_op jit(solution)/shard_map/ppermute | solution.py:66
  613.8 6.8 collective-permute-done.13
  620.6 10.6 %collective-permute-done.15 = bf16[128,2048]{1,0:T(8,128)(2,1)} collective-permute-done((bf16[128,2048]{1,0:T(8,128)(2,1)}, bf16[128,2048]{1,0:T(8,128)(2,1)}, u32[]{:S(2)}, u32[]{:S(2)}) %collective-permute-start.15) | collective-permute-done | bytes 524320 | tf_op jit(solution)/shard_map/ppermute | solution.py:66
  642.7 53.2 %psum.7 = f32[4352]{0:T(1024)S(1)} all-reduce(f32[4352]{0:T(1024)S(1)} %pad_maximum_fusion.15), channel_id=1, replica_groups=mesh['dp'=2,'ctx'=4,'tensor'=4] {'dp','ctx','tensor'}, use_global_device_ids=true, to_apply=%region_26.27 | all-reduce | flops 4352 | bytes 34816 | tf_op jit(solution)/shard_map/psum | solution.py:315
  702.3 10.7 %collective-permute-done.18 = bf16[128,2048]{1,0:T(8,128)(2,1)S(1)} collective-permute-done((bf16[128,2048]{1,0:T(8,128)(2,1)}, bf16[128,2048]{1,0:T(8,128)(2,1)S(1)}, u32[]{:S(2)}, u32[]{:S(2)}) %collective-permute-start.18) | collective-permute-done | bytes 524320 | tf_op jit(solution)/shard_map/ppermute | solution.py:66
  713.0 9.3 %collective-permute-done.17 = bf16[128,2048]{1,0:T(8,128)(2,1)S(1)} collective-permute-done((bf16[128,2048]{1,0:T(8,128)(2,1)}, bf16[128,2048]{1,0:T(8,128)(2,1)S(1)}, u32[]{:S(2)}, u32[]{:S(2)}) %collective-permute-start.17) | collective-permute-done | bytes 524320 | tf_op jit(solution)/shard_map/ppermute | solution.py:66
  732.4 14.6 %reduce-scatter.13.cloned.1.call-done = bf16[256,1536]{1,0:T(8,128)(2,1)} async-done(((bf16[1024,1536]{1,0:T(8,128)(2,1)}), bf16[256,1536]{1,0:T(8,128)(2,1)}) %reduce-scatter.13.cloned.1.call-update) | async-done | bytes 786448 | tf_op jit(solution)/shard_map/reduce_scatter | solution.py:104
  749.5 43.4 %reduce-scatter.9.cloned.1.call-done = bf16[256,1024]{1,0:T(8,128)(2,1)} async-done(((bf16[1024,1024]{1,0:T(8,128)(2,1)}), bf16[256,1024]{1,0:T(8,128)(2,1)}) %reduce-scatter.9.cloned.1.call-update) | async-done | bytes 524304 | tf_op jit(solution)/shard_map/reduce_scatter | solution.py:104
  (403 shorter events, 258.3 us)
Async XLA Ops:
  7.2 53.6 %all-gather.7.cloned.1.call-start = ((), (), s32[]{:S(2)}) async-start(), calls=%async_computation.6 | async-start | bytes 4718592 | tf_op jit(solution)/shard_map/all_gather | solution.py:153
  9.2 233.6 %all-gather.9.cloned.1.call-start = ((), (), s32[]{:S(2)}) async-start(), calls=%async_computation.7 | async-start | bytes 2621440 | tf_op jit(solution)/shard_map/all_gather | solution.py:221
  73.2 193.9 %all-gather.11.cloned.1.call-start = ((), (), s32[]{:S(2)}) async-start(), calls=%async_computation.8 | async-start | bytes 2359296 | tf_op jit(solution)/shard_map/all_gather | solution.py:156
  73.9 232.4 %all-gather.15.cloned.1.call-start = ((), (), s32[]{:S(2)}) async-start(), calls=%async_computation.10 | async-start | bytes 7077888 | tf_op jit(solution)/shard_map/all_gather | solution.py:171
  74.5 293.5 %all-gather.13.cloned.1.call-start = ((), (), s32[]{:S(2)}) async-start(), calls=%async_computation.9 | async-start | bytes 7077888 | tf_op jit(solution)/shard_map/all_gather | solution.py:170
  74.6 33.2 %collective-permute-start.6 = (bf16[256,1536]{1,0:T(8,128)(2,1)}, bf16[256,1536]{1,0:T(8,128)(2,1)}, u32[]{:S(2)}, u32[]{:S(2)}) collective-permute-start(bf16[256,1536]{1,0:T(8,128)(2,1)} %param.22), channel_id=1, source_target_pairs={{0,4},{4,8},{8,12},{12,16},{16,20},{20,24},{24,28},{28,0},{1,5},{5... | collective-permute-start | bytes 2359304 | tf_op jit(solution)/shard_map/ppermute | solution.py:163
  107.8 38.4 %collective-permute-start.7 = (bf16[256,1536]{1,0:T(8,128)(2,1)}, bf16[256,1536]{1,0:T(8,128)(2,1)}, u32[]{:S(2)}, u32[]{:S(2)}) collective-permute-start(bf16[256,1536]{1,0:T(8,128)(2,1)} %collective-permute-done.6), channel_id=1, source_target_pairs={{0,4},{4,8},{8,12},{12,16},{16,20},{20,24},{24,28},{28,0},{1,5},{5... | collective-permute-start | bytes 2359304 | tf_op jit(solution)/shard_map/ppermute | solution.py:163
  118.1 49.8 %collective-permute-start.10 = (bf16[256,1536]{1,0:T(8,128)(2,1)}, bf16[256,1536]{1,0:T(8,128)(2,1)}, u32[]{:S(2)}, u32[]{:S(2)}) collective-permute-start(bf16[256,1536]{1,0:T(8,128)(2,1)} %param.22), channel_id=1, source_target_pairs={{4,0},{8,4},{12,8},{16,12},{20,16},{24,20},{28,24},{0,28},{5,1},{9... | collective-permute-start | bytes 2359304 | tf_op jit(solution)/shard_map/ppermute | solution.py:165
  118.1 442.4 %reduce-scatter.7.cloned.1.call-start = ((), (), s32[]{:S(2)}) async-start(), calls=%async_computation.11 | async-start | bytes 2621440 | tf_op jit(solution)/shard_map/reduce_scatter | solution.py:280
  146.2 48.6 %collective-permute-start.8 = (bf16[256,1536]{1,0:T(8,128)(2,1)}, bf16[256,1536]{1,0:T(8,128)(2,1)}, u32[]{:S(2)}, u32[]{:S(2)}) collective-permute-start(bf16[256,1536]{1,0:T(8,128)(2,1)} %collective-permute-done.7), channel_id=1, source_target_pairs={{0,4},{4,8},{8,12},{12,16},{16,20},{20,24},{24,28},{28,0},{1,5},{5... | collective-permute-start | bytes 2359304 | tf_op jit(solution)/shard_map/ppermute | solution.py:163
  167.9 47.6 %collective-permute-start.11 = (bf16[256,1536]{1,0:T(8,128)(2,1)}, bf16[256,1536]{1,0:T(8,128)(2,1)}, u32[]{:S(2)}, u32[]{:S(2)}) collective-permute-start(bf16[256,1536]{1,0:T(8,128)(2,1)} %collective-permute-done.10), channel_id=1, source_target_pairs={{4,0},{8,4},{12,8},{16,12},{20,16},{24,20},{28,24},{0,28},{5,1},{9... | collective-permute-start | bytes 2359304 | tf_op jit(solution)/shard_map/ppermute | solution.py:165
  194.8 36.6 %collective-permute-start.9 = (bf16[256,1536]{1,0:T(8,128)(2,1)}, bf16[256,1536]{1,0:T(8,128)(2,1)S(1)}, u32[]{:S(2)}, u32[]{:S(2)}) collective-permute-start(bf16[256,1536]{1,0:T(8,128)(2,1)} %collective-permute-done.8), channel_id=1, source_target_pairs={{0,4},{4,8},{8,12},{12,16},{16,20},{20,24},{24,28},{28,0},{1,5},{5... | collective-permute-start | bytes 2359304 | tf_op jit(solution)/shard_map/ppermute | solution.py:163
  215.5 63.5 %collective-permute-start.12 = (bf16[256,1536]{1,0:T(8,128)(2,1)}, bf16[256,1536]{1,0:T(8,128)(2,1)}, u32[]{:S(2)}, u32[]{:S(2)}) collective-permute-start(bf16[256,1536]{1,0:T(8,128)(2,1)} %collective-permute-done.11), channel_id=1, source_target_pairs={{4,0},{8,4},{12,8},{16,12},{20,16},{24,20},{28,24},{0,28},{5,1},{9... | collective-permute-start | bytes 2359304 | tf_op jit(solution)/shard_map/ppermute | solution.py:165
  275.4 23.6 %collective-permute-start.1 = (bf16[128,2048]{1,0:T(8,128)(2,1)}, bf16[128,2048]{1,0:T(8,128)(2,1)S(1)}, u32[]{:S(2)}, u32[]{:S(2)}) collective-permute-start(bf16[128,2048]{1,0:T(8,128)(2,1)} %get-tuple-element.82), channel_id=1, source_target_pairs={{0,2},{1,3},{2,0},{3,1},{4,6},{5,7},{6,4},{7,5},{8,10},{9,11},{10,... | collective-permute-start | bytes 1572872 | tf_op jit(solution)/shard_map/ppermute | solution.py:66
  302.3 65.7 %collective-permute-start.5 = (bf16[128,2048]{1,0:T(8,128)(2,1)S(1)}, bf16[128,2048]{1,0:T(8,128)(2,1)}, u32[]{:S(2)}, u32[]{:S(2)}) collective-permute-start(bf16[128,2048]{1,0:T(8,128)(2,1)S(1)} %multiply_convert_fusion.4), channel_id=1, source_target_pairs={{0,3},{1,2},{2,1},{3,0},{4,7},{5,6},{6,5},{7,4},{8,11},{9,10},{10,... | collective-permute-start | bytes 1572872 | tf_op jit(solution)/shard_map/ppermute | solution.py:66
  302.4 65.6 %collective-permute-start.4 = (bf16[128,2048]{1,0:T(8,128)(2,1)S(1)}, bf16[128,2048]{1,0:T(8,128)(2,1)}, u32[]{:S(2)}, u32[]{:S(2)}) collective-permute-start(bf16[128,2048]{1,0:T(8,128)(2,1)S(1)} %multiply_convert_fusion.4), channel_id=1, source_target_pairs={{0,2},{1,3},{2,0},{3,1},{4,6},{5,7},{6,4},{7,5},{8,10},{9,11},{10,... | collective-permute-start | bytes 1572872 | tf_op jit(solution)/shard_map/ppermute | solution.py:66
  304.9 63.1 %collective-permute-start.3 = (bf16[128,2048]{1,0:T(8,128)(2,1)S(1)}, bf16[128,2048]{1,0:T(8,128)(2,1)}, u32[]{:S(2)}, u32[]{:S(2)}) collective-permute-start(bf16[128,2048]{1,0:T(8,128)(2,1)S(1)} %multiply_convert_fusion.4), channel_id=1, source_target_pairs={{0,1},{1,0},{2,3},{3,2},{4,5},{5,4},{6,7},{7,6},{8,9},{9,8},{10,11... | collective-permute-start | bytes 1572872 | tf_op jit(solution)/shard_map/ppermute | solution.py:66
  392.4 24.8 %collective-permute-start.21 = (bf16[128,2048]{1,0:T(8,128)(2,1)S(1)}, bf16[128,2048]{1,0:T(8,128)(2,1)S(1)}, u32[]{:S(2)}, u32[]{:S(2)}) collective-permute-start(bf16[128,2048]{1,0:T(8,128)(2,1)S(1)} %get-tuple-element.67), channel_id=1, source_target_pairs={{0,3},{1,2},{2,1},{3,0},{4,7},{5,6},{6,5},{7,4},{8,11},{9,10},{10,... | collective-permute-start | bytes 1572872 | tf_op jit(solution)/shard_map/ppermute | solution.py:66
  393.9 24.7 %collective-permute-start.20 = (bf16[128,2048]{1,0:T(8,128)(2,1)S(1)}, bf16[128,2048]{1,0:T(8,128)(2,1)S(1)}, u32[]{:S(2)}, u32[]{:S(2)}) collective-permute-start(bf16[128,2048]{1,0:T(8,128)(2,1)S(1)} %get-tuple-element.68), channel_id=1, source_target_pairs={{0,2},{1,3},{2,0},{3,1},{4,6},{5,7},{6,4},{7,5},{8,10},{9,11},{10,... | collective-permute-start | bytes 1572872 | tf_op jit(solution)/shard_map/ppermute | solution.py:66
  489.4 151.2 %reduce-scatter.11.cloned.1.call-start = ((), (), s32[]{:S(2)}) async-start(), calls=%async_computation.13 | async-start | bytes 1310720 | tf_op jit(solution)/shard_map/reduce_scatter | solution.py:104
  505.6 221.4 %reduce-scatter.17.cloned.1.call-start = ((), (), s32[]{:S(2)}) async-start(), calls=%async_computation.16 | async-start | bytes 3932160 | tf_op jit(solution)/shard_map/reduce_scatter | solution.py:104
  511.9 218.0 %reduce-scatter.15.cloned.1.call-start = ((), (), s32[]{:S(2)}) async-start(), calls=%async_computation.15 | async-start | bytes 3932160 | tf_op jit(solution)/shard_map/reduce_scatter | solution.py:104
  525.3 221.7 %reduce-scatter.13.cloned.1.call-start = ((), (), s32[]{:S(2)}) async-start(), calls=%async_computation.14 | async-start | bytes 3932160 | tf_op jit(solution)/shard_map/reduce_scatter | solution.py:104
  543.2 249.7 %reduce-scatter.9.cloned.1.call-start = ((), (), s32[]{:S(2)}) async-start(), calls=%async_computation.12 | async-start | bytes 2621440 | tf_op jit(solution)/shard_map/reduce_scatter | solution.py:104
  583.8 25.7 %collective-permute-start.27 = (bf16[128,2048]{1,0:T(8,128)(2,1)}, bf16[128,2048]{1,0:T(8,128)(2,1)}, u32[]{:S(2)}, u32[]{:S(2)}) collective-permute-start(bf16[128,2048]{1,0:T(8,128)(2,1)} %get-tuple-element.64), channel_id=1, source_target_pairs={{0,3},{1,2},{2,1},{3,0},{4,7},{5,6},{6,5},{7,4},{8,11},{9,10},{10,... | collective-permute-start | bytes 1572872 | tf_op jit(solution)/shard_map/ppermute | solution.py:66
  585.1 26.3 %collective-permute-start.26 = (bf16[128,2048]{1,0:T(8,128)(2,1)}, bf16[128,2048]{1,0:T(8,128)(2,1)}, u32[]{:S(2)}, u32[]{:S(2)}) collective-permute-start(bf16[128,2048]{1,0:T(8,128)(2,1)} %get-tuple-element.65), channel_id=1, source_target_pairs={{0,2},{1,3},{2,0},{3,1},{4,6},{5,7},{6,4},{7,5},{8,10},{9,11},{10,... | collective-permute-start | bytes 1572872 | tf_op jit(solution)/shard_map/ppermute | solution.py:66
  587.6 33.0 %collective-permute-start.13 = (bf16[128,2048]{1,0:T(8,128)(2,1)}, bf16[128,2048]{1,0:T(8,128)(2,1)}, u32[]{:S(2)}, u32[]{:S(2)}) collective-permute-start(bf16[128,2048]{1,0:T(8,128)(2,1)} %get-tuple-element.77), channel_id=1, source_target_pairs={{0,1},{1,0},{2,3},{3,2},{4,5},{5,4},{6,7},{7,6},{8,9},{9,8},{10,11... | collective-permute-start | bytes 1572872 | tf_op jit(solution)/shard_map/ppermute | solution.py:66
  588.4 42.8 %collective-permute-start.15 = (bf16[128,2048]{1,0:T(8,128)(2,1)}, bf16[128,2048]{1,0:T(8,128)(2,1)}, u32[]{:S(2)}, u32[]{:S(2)}) collective-permute-start(bf16[128,2048]{1,0:T(8,128)(2,1)} %get-tuple-element.78), channel_id=1, source_target_pairs={{0,3},{1,2},{2,1},{3,0},{4,7},{5,6},{6,5},{7,4},{8,11},{9,10},{10,... | collective-permute-start | bytes 1572872 | tf_op jit(solution)/shard_map/ppermute | solution.py:66
  597.9 34.5 %collective-permute-start.14 = (bf16[128,2048]{1,0:T(8,128)(2,1)}, bf16[128,2048]{1,0:T(8,128)(2,1)S(1)}, u32[]{:S(2)}, u32[]{:S(2)}) collective-permute-start(bf16[128,2048]{1,0:T(8,128)(2,1)} %get-tuple-element.79), channel_id=1, source_target_pairs={{0,2},{1,3},{2,0},{3,1},{4,6},{5,7},{6,4},{7,5},{8,10},{9,11},{10,... | collective-permute-start | bytes 1572872 | tf_op jit(solution)/shard_map/ppermute | solution.py:66
  637.1 63.7 %collective-permute-start.30 = (bf16[128,2048]{1,0:T(8,128)(2,1)}, bf16[128,2048]{1,0:T(8,128)(2,1)S(1)}, u32[]{:S(2)}, u32[]{:S(2)}) collective-permute-start(bf16[128,2048]{1,0:T(8,128)(2,1)} %get-tuple-element.91), channel_id=1, source_target_pairs={{0,3},{1,2},{2,1},{3,0},{4,7},{5,6},{6,5},{7,4},{8,11},{9,10},{10,... | collective-permute-start | bytes 1572872 | tf_op jit(solution)/shard_map/ppermute | solution.py:66
  638.7 62.1 %collective-permute-start.29 = (bf16[128,2048]{1,0:T(8,128)(2,1)}, bf16[128,2048]{1,0:T(8,128)(2,1)S(1)}, u32[]{:S(2)}, u32[]{:S(2)}) collective-permute-start(bf16[128,2048]{1,0:T(8,128)(2,1)} %get-tuple-element.91), channel_id=1, source_target_pairs={{0,2},{1,3},{2,0},{3,1},{4,6},{5,7},{6,4},{7,5},{8,10},{9,11},{10,... | collective-permute-start | bytes 1572872 | tf_op jit(solution)/shard_map/ppermute | solution.py:66
  640.1 60.8 %collective-permute-start.28 = (bf16[128,2048]{1,0:T(8,128)(2,1)}, bf16[128,2048]{1,0:T(8,128)(2,1)S(1)}, u32[]{:S(2)}, u32[]{:S(2)}) collective-permute-start(bf16[128,2048]{1,0:T(8,128)(2,1)} %get-tuple-element.91), channel_id=1, source_target_pairs={{0,1},{1,0},{2,3},{3,2},{4,5},{5,4},{6,7},{7,6},{8,9},{9,8},{10,11... | collective-permute-start | bytes 1572872 | tf_op jit(solution)/shard_map/ppermute | solution.py:66
  (99 other events, 2014.5 us)
Sparse Core Ops, SparseCore 0:
  10.2 50.5 all-gather.6
  73.3 79.5 all-gather.8
  154.5 51.9 all-gather.10
  208.0 92.8 all-gather.14
  302.4 65.5 all-gather.12
  489.6 41.3 reduce-scatter.6
  533.2 26.4 reduce-scatter.10
  562.1 58.9 reduce-scatter.16
  623.3 61.0 reduce-scatter.14
  686.6 60.4 reduce-scatter.12
  749.3 43.5 reduce-scatter.8
